TPU v7x, 32 devices: a whole 2x2x4 slice. The times are simulated.
32 devices in a mesh: dp: 8 (over y, x, core), tensor: 4 (over z).
Axes of the slice: x: 2, y: 2, z: 4, core: 2. Of those that a mesh axis runs over, the one named last changes fastest.
Arguments:
- tokens: bfloat16 [4096, 4096], P(('dp', 'tensor')), may hold values from -120 to 120
- norm_gain: float32 [4096], replicated, may hold values from 0.5 to 1.5
- w_gate: bfloat16 [4096, 8192], P('dp', 'tensor'), may hold values from -0.09375 to 0.09375
- w_up: bfloat16 [4096, 8192], P('dp', 'tensor'), may hold values from -0.09375 to 0.09375
- probes: bfloat16 [4096, 2, 8192], P('dp', None, 'tensor'), may hold values from -0.09375 to 0.09375
- cotangent: bfloat16 [4096, 8192], P('dp', 'tensor'), may hold values from -6 to 6
Outputs:
- hvp: float32 [4096, 2, 8192], P('dp', None, 'tensor')
All inputs are finite; a program needn't handle non-finite values.
Results may differ from a plain program's by a relative error of at most 0.014.
Values may be sent and summed in bfloat16 or wider, within the bound.
A program may use at most 128 MiB of HBM per device.

v0:
```python
import math
import jax
import jax.numpy as jnp
from jax import lax
from jax.sharding import PartitionSpec as P


def normalize(tokens, norm_gain):
    values = tokens.astype(jnp.float32)
    inverse = lax.rsqrt(jnp.mean(values * values, axis=1, keepdims=True) + 1e-05)
    return (values * inverse * norm_gain).astype(jnp.bfloat16)


def curvature(gate_pre):
    logistic = jax.nn.sigmoid(gate_pre)
    return logistic * (1.0 - logistic) * (2.0 + gate_pre * (1.0 - 2.0 * logistic))


def per_device(tokens, norm_gain, w_gate, w_up, probes, cotangent):
    normed = lax.all_gather(normalize(tokens, norm_gain), "tensor", axis=0, tiled=True)
    row_count = normed.shape[0]
    local_depth, probe_count, local_units = probes.shape
    probe_width = probe_count * local_units

    def project(shard_piece):
        return jnp.dot(normed, shard_piece, preferred_element_type=jnp.float32)

    gate_pre = project(lax.all_gather(w_gate, "dp", axis=0, tiled=True))
    up_pre = project(lax.all_gather(w_up, "dp", axis=0, tiled=True))
    shard_piece = lax.all_gather(probes, "dp", axis=0, tiled=True)
    tangent = project(shard_piece.reshape(shard_piece.shape[0], probe_width))
    scale_factor = 1.0 / math.sqrt(row_count * lax.axis_size("dp"))
    weighting = cotangent.astype(jnp.float32) * curvature(gate_pre) * up_pre * scale_factor
    second = (weighting[:, None, :] * tangent.reshape(row_count, probe_count, local_units)).astype(
        jnp.bfloat16
    )
    second = second.reshape(row_count, probe_width)
    result = lax.psum_scatter(
        lax.dot_general(
            normed, second, (((0,), (0,)), ((), ())), preferred_element_type=jnp.float32
        ).astype(jnp.bfloat16),
        "dp",
        scatter_dimension=0,
        tiled=True,
    ).astype(jnp.float32)
    return result.reshape(local_depth, probe_count, local_units)


def solution(mesh):
    in_specs = (
        P(("dp", "tensor"), None),
        P(),
        P("dp", "tensor"),
        P("dp", "tensor"),
        P("dp", None, "tensor"),
        P("dp", "tensor"),
    )
    out_specs = P("dp", None, "tensor")
    return jax.shard_map(
        per_device, mesh=mesh, in_specs=in_specs, out_specs=out_specs, check_vma=False
    )
```

profile of v0, /device:TPU:0, one launch (start us, length us, event | category | flops | bytes accessed | tf_op | source)
XLA Modules:
  0.0 797.4 jit_solution(14628051146677067251)
XLA Ops:
  6.5 0.0 all-gather.5.cloned.1.call-start
  6.5 1.5 fusion.11
  8.1 2.5 fusion.13
  10.6 0.0 all-gather.5.cloned.1.call-update
  10.6 0.0 all-gather.7.cloned.1.call-start
  10.7 0.7 all-gather.7.cloned.1.call-update
  11.4 0.0 all-gather.9.cloned.1.call-start
  11.4 0.7 all-gather.9.cloned.1.call-update
  12.1 0.0 all-gather.11.cloned.1.call-start
  12.2 0.5 all-gather.11.cloned.1.call-update
  12.7 0.0 copy-start
  12.7 0.0 reduce-scatter.2.cloned.1.call-start
  12.7 81.5 %all-gather.5.cloned.1.call-done = bf16[512,4096]{1,0:T(8,128)(2,1)} async-done(((bf16[128,4096]{1,0:T(8,128)(2,1)}), bf16[512,4096]{1,0:T(8,128)(2,1)}) %all-gather.5.cloned.1.call-update) | async-done | bytes 4194320 | tf_op jit(solution)/shard_map/all_gather | solution.py:20
  94.2 90.1 %all-gather.7.cloned.1.call-done = bf16[4096,2048]{1,0:T(8,128)(2,1)} async-done(((bf16[512,2048]{1,0:T(8,128)(2,1)}), bf16[4096,2048]{1,0:T(8,128)(2,1)}) %all-gather.7.cloned.1.call-update) | async-done | bytes 16777232 | tf_op jit(solution)/shard_map/all_gather | solution.py:28
  184.4 14.9 %fusion.14 = f32[512,2048]{1,0:T(8,128)} fusion(bf16[512,4096]{1,0:T(8,128)(2,1)} %all-gather.5.cloned.1.call-done, bf16[4096,2048]{1,0:T(8,128)(2,1)} %all-gather.7.cloned.1.call-done), kind=kOutput, calls=%fused_computation.16 | convolution fusion | flops 8589934592 | bytes 25165824 | tf_op jit(solution)/shard_map/dot_general | solution.py:26
  199.3 76.8 %all-gather.9.cloned.1.call-done = bf16[4096,2048]{1,0:T(8,128)(2,1)} async-done(((bf16[512,2048]{1,0:T(8,128)(2,1)}), bf16[4096,2048]{1,0:T(8,128)(2,1)}) %all-gather.9.cloned.1.call-update) | async-done | bytes 16777232 | tf_op jit(solution)/shard_map/all_gather | solution.py:29
  276.0 0.0 copy-done
  276.0 17.0 %fusion.5 = f32[512,2048]{1,0:T(8,128)} fusion(f32[512,2048]{1,0:T(8,128)} %fusion.14, bf16[512,2048]{1,0:T(8,128)(2,1)S(1)} %copy-done, bf16[512,4096]{1,0:T(8,128)(2,1)} %all-gather.5.cloned.1.call-done, bf16[4096,2048]{1,0:T(8,128)(2,1)} %all-gather.9.cloned.1.call-done), kind=kOutput, calls=%fused_computation.8 | convolution fusion | flops 8604614656 | bytes 31457280 | tf_op jit(solution)/shard_map/dot_general | solution.py:26
  293.0 145.5 %all-gather.11.cloned.1.call-done = bf16[4096,2,2048]{2,1,0:T(2,128)(2,1)} async-done(((bf16[512,2,2048]{2,1,0:T(2,128)(2,1)}), bf16[4096,2,2048]{2,1,0:T(2,128)(2,1)}) %all-gather.11.cloned.1.call-update) | async-done | bytes 33554448 | tf_op jit(solution)/shard_map/all_gather | solution.py:30
  438.5 80.7 %copy.12 = bf16[4096,2,2048]{0,2,1:T(8,128)(2,1)} copy(bf16[4096,2,2048]{2,1,0:T(2,128)(2,1)} %all-gather.11.cloned.1.call-done) | data formatting | bytes 67108864 | tf_op jit(solution)/shard_map/reshape | solution.py:31
  519.2 24.2 %multiply_convert_fusion = bf16[512,2,2048]{2,0,1:T(8,128)(2,1)} fusion(f32[512,2048]{1,0:T(8,128)} %fusion.5, bf16[4096,2,2048]{0,2,1:T(8,128)(2,1)} %copy.12, bf16[512,4096]{1,0:T(8,128)(2,1)} %all-gather.5.cloned.1.call-done), kind=kOutput, calls=%fused_computation.3 | convolution fusion | flops 17184063488 | bytes 46137344 | tf_op jit(solution)/shard_map/dot_general | solution.py:26
  543.4 6.2 copy.11
  549.6 24.1 %convolution_convert_fusion = bf16[4096,4096]{1,0:T(8,128)(2,1)} fusion(bf16[512,4096]{1,0:T(8,128)(2,1)} %all-gather.5.cloned.1.call-done, bf16[512,4096]{0,1:T(8,128)(2,1)} %bitcast.21), kind=kOutput, calls=%fused_computation.2 | convolution fusion | flops 17196646400 | bytes 41943040 | tf_op jit(solution)/shard_map/dot_general | solution.py:39
  573.7 0.0 reduce-scatter.2.cloned.1.call-update
  573.7 205.6 %reduce-scatter.2.cloned.1.call-done = bf16[512,4096]{1,0:T(8,128)(2,1)} async-done(((bf16[4096,4096]{1,0:T(8,128)(2,1)}), bf16[512,4096]{1,0:T(8,128)(2,1)}) %reduce-scatter.2.cloned.1.call-update) | async-done | bytes 4194320 | tf_op jit(solution)/shard_map/reduce_scatter | solution.py:38
  779.4 11.5 %reshape.29 = f32[512,2,2048]{2,1,0:T(2,128)} reshape(bf16[512,4096]{1,0:T(8,128)(2,1)} %reduce-scatter.2.cloned.1.call-done) | data formatting | bytes 12582912 | tf_op jit(solution)/shard_map/reshape | solution.py:46
  (1 shorter events, 0.0 us)
Async XLA Ops:
  6.5 87.7 %all-gather.5.cloned.1.call-start = ((), (), s32[]{:S(2)}) async-start(), calls=%async_computation.1 | async-start | bytes 5242880 | tf_op jit(solution)/shard_map/all_gather | solution.py:20
  10.6 173.8 %all-gather.7.cloned.1.call-start = ((), (), s32[]{:S(2)}) async-start(), calls=%async_computation.2 | async-start | bytes 18874368 | tf_op jit(solution)/shard_map/all_gather | solution.py:28
  11.4 264.7 %all-gather.9.cloned.1.call-start = ((), (), s32[]{:S(2)}) async-start(), calls=%async_computation.3 | async-start | bytes 18874368 | tf_op jit(solution)/shard_map/all_gather | solution.py:29
  12.1 426.4 %all-gather.11.cloned.1.call-start = ((), (), s32[]{:S(2)}) async-start(), calls=%async_computation.4 | async-start | bytes 37748736 | tf_op jit(solution)/shard_map/all_gather | solution.py:30
  12.7 263.3 %copy-start = (bf16[512,2048]{1,0:T(8,128)(2,1)S(1)}, bf16[512,2048]{1,0:T(8,128)(2,1)}, u32[]{:S(2)}) copy-start(bf16[512,2048]{1,0:T(8,128)(2,1)} %param.11) | copy-start | bytes 6291460
  12.7 766.7 %reduce-scatter.2.cloned.1.call-start = ((), (), s32[]{:S(2)}) async-start(), calls=%async_computation.5 | async-start | bytes 37748736 | tf_op jit(solution)/shard_map/reduce_scatter | solution.py:38
Sparse Core Ops, SparseCore 0:
  10.7 83.4 all-gather.4
  96.1 88.2 all-gather.6
  186.3 89.7 all-gather.8
  277.8 160.6 all-gather.10
  573.9 205.4 reduce-scatter.1
where the time goes:
time: 800 us; the launch traced here: 797 us
  waiting for transfers between devices  601 us (75%)
  local copies, waits for them, and re-layouts  98.4 us (12%)
  matrix products  80.2 us (10%)
  between operations  13.2 us (2%)
    reduce_scatter x1, waiting for transfers between devices, per_device(): lax.psum_scatter(lax.dot_general(normed, second, (((0,), (0,)), ((), ()))...  206 us
    all_gather x1, waiting for transfers between devices, per_device(): shard_piece = lax.all_gather(probes, 'dp', axis=0, tiled=True)  145 us
    all_gather x1, waiting for transfers between devices, per_device(): gate_pre = project(lax.all_gather(w_gate, 'dp', axis=0, tiled=True))  90.1 us
    all_gather x1, waiting for transfers between devices, per_device(): lax.all_gather(normalize(tokens, norm_gain), 'tensor', axis=0, tiled=True)  81.5 us
    reshape x1, local copies, waits for them, and re-layouts, per_device(): tangent = project(shard_piece.reshape(shard_piece.shape[0], probe_width))  80.7 us
    all_gather x1, waiting for transfers between devices, per_device(): up_pre = project(lax.all_gather(w_up, 'dp', axis=0, tiled=True))  76.8 us
    dot_general x3, matrix products, project(): return jnp.dot(normed, shard_piece, preferred_element_type=jnp.float32)  56.1 us
    dot_general x1, matrix products, per_device(): lax.dot_general(normed, second, (((0,), (0,)), ((), ())), preferred_eleme...  24.1 us
  transfers between devices with their start and end apart: 5, of which 5 were waited for; matrix products, arithmetic and copies ran while one was open for 4% of the time, Pallas kernels for 0%

commit v1 on v0

--- a/solution.py
+++ b/solution.py
@@ -3,6 +3,22 @@
 import jax.numpy as jnp
 from jax import lax
 from jax.sharding import PartitionSpec as P
+
+
+def gather_around(x, axis, dim):
+    ways, here, hop = (lax.axis_size(axis), lax.axis_index(axis), x.shape[dim])
+    dims = [n * ways if d == dim else n for d, n in enumerate(x.shape)]
+    full = lax.dynamic_update_slice_in_dim(jnp.zeros(dims, x.dtype), x, here * hop, axis=dim)
+    going_up = going_down = x
+    for far in range(1, ways // 2 + 1):
+        going_up = lax.ppermute(going_up, axis, [(d, (d + 1) % ways) for d in range(ways)])
+        full = lax.dynamic_update_slice_in_dim(full, going_up, (here - far) % ways * hop, axis=dim)
+        if 2 * far < ways:
+            going_down = lax.ppermute(going_down, axis, [(d, (d - 1) % ways) for d in range(ways)])
+            full = lax.dynamic_update_slice_in_dim(
+                full, going_down, (here + far) % ways * hop, axis=dim
+            )
+    return full
 
 
 def normalize(tokens, norm_gain):
@@ -25,7 +41,7 @@
     def project(shard_piece):
         return jnp.dot(normed, shard_piece, preferred_element_type=jnp.float32)
 
-    gate_pre = project(lax.all_gather(w_gate, "dp", axis=0, tiled=True))
+    gate_pre = project(gather_around(w_gate, "dp", 0))
     up_pre = project(lax.all_gather(w_up, "dp", axis=0, tiled=True))
     shard_piece = lax.all_gather(probes, "dp", axis=0, tiled=True)
     tangent = project(shard_piece.reshape(shard_piece.shape[0], probe_width))

time: 800 us -> 761 us (0.951)
  waiting for transfers between devices: 601 us -> 526 us
  local copies, waits for them, and re-layouts: 98.4 us -> 124 us
  starting transfers between devices: 0.16 us -> 11.1 us
    ppermute x0 -> x7, waiting for transfers between devices: none -> 197 us  [the longest x4 188 us: gather_around(): lax.ppermute(going_up, axis, [(d, (d + 1) % ways) for d in range(ways)])]
    all_gather x1 -> x0, waiting for transfers between devices: 90.1 us -> none  [per_device(): gate_pre = project(lax.all_gather(w_gate, 'dp', axis=0, tiled=True))]
    all_gather x1, waiting for transfers between devices: 81.5 us -> 0.01 us  [per_device(): lax.all_gather(normalize(tokens, norm_gain), 'tensor', axis=0, tiled=True)]
    all_gather x1, waiting for transfers between devices: 76.8 us -> 0.01 us  [per_device(): up_pre = project(lax.all_gather(w_up, 'dp', axis=0, tiled=True))]
    all_gather x1, waiting for transfers between devices: 145 us -> 122 us  [per_device(): shard_piece = lax.all_gather(probes, 'dp', axis=0, tiled=True)]
    dynamic_update_slice x0 -> x8, local copies, waits for them, and re-layouts: none -> 18.6 us  [the longest x4 9.27 us: gather_around(): lax.dynamic_update_slice_in_dim(full, going_up, (here - far) % ways * hop...]
    ppermute x0 -> x7, starting transfers between devices: none -> 11 us  [the longest x3 9.05 us: gather_around(): lax.ppermute(going_down, axis, [(d, (d - 1) % ways) for d in range(ways)])]
  transfers between devices with their start and end apart: 5 -> 11, of which waited for: 5 -> 8; matrix products, arithmetic and copies ran while one was open for 4% -> 7% of each run, Pallas kernels for 0% -> 0%
where the time goes in v1:
time: 761 us; the launch traced here: 758 us
  waiting for transfers between devices  526 us (69%)
  local copies, waits for them, and re-layouts  124 us (16%)
  matrix products  79.5 us (10%)
  between operations  13.2 us (2%)
  starting transfers between devices  11.1 us (1%)
    reduce_scatter x1, waiting for transfers between devices, per_device(): lax.psum_scatter(lax.dot_general(normed, second, (((0,), (0,)), ((), ()))...  206 us
    ppermute x4, waiting for transfers between devices, gather_around(): lax.ppermute(going_up, axis, [(d, (d + 1) % ways) for d in range(ways)])  188 us
    all_gather x1, waiting for transfers between devices, per_device(): shard_piece = lax.all_gather(probes, 'dp', axis=0, tiled=True)  122 us
    reshape x1, local copies, waits for them, and re-layouts, per_device(): tangent = project(shard_piece.reshape(shard_piece.shape[0], probe_width))  80.8 us
    dot_general x3, matrix products, project(): return jnp.dot(normed, shard_piece, preferred_element_type=jnp.float32)  55.3 us
    dot_general x1, matrix products, per_device(): lax.dot_general(normed, second, (((0,), (0,)), ((), ())), preferred_eleme...  24.2 us
  transfers between devices with their start and end apart: 11, of which 8 were waited for; matrix products, arithmetic and copies ran while one was open for 7% of the time, Pallas kernels for 0%

profile of v1, /device:TPU:0, one launch (start us, length us, event | category | flops | bytes accessed | tf_op | source)
XLA Modules:
  0.0 758.2 jit_solution(4498429646615686772)
XLA Ops:
  6.5 0.0 all-gather.4.cloned.1.call-start
  6.5 1.5 fusion.11
  8.1 2.5 fusion.13
  10.6 0.0 copy-start
  10.6 0.0 all-gather.4.cloned.1.call-update
  10.6 0.0 all-gather.6.cloned.1.call-start
  10.7 0.7 all-gather.6.cloned.1.call-update
  11.4 0.0 all-gather.8.cloned.1.call-start
  11.4 0.7 all-gather.8.cloned.1.call-update
  12.1 0.0 reduce-scatter.2.cloned.1.call-start
  12.2 0.0 copy-done
  12.2 0.5 collective-permute-start
  12.7 2.9 collective-permute-start.1
  15.7 43.5 %collective-permute-done = bf16[512,2048]{1,0:T(8,128)(2,1)S(1)} collective-permute-done((bf16[512,2048]{1,0:T(8,128)(2,1)S(1)}, bf16[512,2048]{1,0:T(8,128)(2,1)S(1)}, u32[]{:S(2)}, u32[]{:S(2)}) %collective-permute-start) | collective-permute-done | bytes 2097184 | tf_op jit(solution)/shard_map/ppermute | solution.py:14
  59.2 0.0 copy-start.1
  59.2 0.5 collective-permute-start.2
  59.7 0.9 collective-permute-done.1
  60.7 0.0 copy-done.1
  60.7 0.0 copy-start.3
  60.7 3.2 collective-permute-start.3
  63.9 41.5 %collective-permute-done.2 = bf16[512,2048]{1,0:T(8,128)(2,1)S(1)} collective-permute-done((bf16[512,2048]{1,0:T(8,128)(2,1)S(1)}, bf16[512,2048]{1,0:T(8,128)(2,1)S(1)}, u32[]{:S(2)}, u32[]{:S(2)}) %collective-permute-start.2) | collective-permute-done | bytes 2097184 | tf_op jit(solution)/shard_map/ppermute | solution.py:14
  105.4 0.0 copy-done.3
  105.4 0.0 copy-start.5
  105.4 0.9 collective-permute-start.4
  106.3 8.2 %collective-permute-done.3 = bf16[512,2048]{1,0:T(8,128)(2,1)} collective-permute-done((bf16[512,2048]{1,0:T(8,128)(2,1)S(1)}, bf16[512,2048]{1,0:T(8,128)(2,1)}, u32[]{:S(2)}, u32[]{:S(2)}) %collective-permute-start.3) | collective-permute-done | bytes 2097184 | tf_op jit(solution)/shard_map/ppermute | solution.py:17
  114.5 0.0 copy-done.5
  114.6 2.9 collective-permute-start.5
  117.5 73.1 %collective-permute-done.4 = bf16[512,2048]{1,0:T(8,128)(2,1)} collective-permute-done((bf16[512,2048]{1,0:T(8,128)(2,1)S(1)}, bf16[512,2048]{1,0:T(8,128)(2,1)}, u32[]{:S(2)}, u32[]{:S(2)}) %collective-permute-start.4) | collective-permute-done | bytes 2097184 | tf_op jit(solution)/shard_map/ppermute | solution.py:14
  190.5 0.0 collective-permute-start.6
  190.5 6.0 broadcast_in_dim.2
  196.5 0.0 copy-start.2
  196.5 0.0 copy-start.4
  196.5 1.4 constant_dynamic-update-slice_fusion.7
  198.0 0.9 copy-done.2
  198.9 0.0 copy-start.6
  198.9 1.4 constant_dynamic-update-slice_fusion.6
  200.3 0.0 copy-done.4
  200.3 1.5 constant_dynamic-update-slice_fusion.5
  201.8 0.0 copy-done.6
  201.8 1.5 constant_dynamic-update-slice_fusion.4
  203.3 3.2 constant_dynamic-update-slice_fusion.3
  206.5 3.2 constant_dynamic-update-slice_fusion.2
  209.6 0.0 collective-permute-done.5
  209.6 3.2 constant_dynamic-update-slice_fusion.1
  212.8 30.1 %collective-permute-done.6 = bf16[512,2048]{1,0:T(8,128)(2,1)} collective-permute-done((bf16[512,2048]{1,0:T(8,128)(2,1)}, bf16[512,2048]{1,0:T(8,128)(2,1)}, u32[]{:S(2)}, u32[]{:S(2)}) %collective-permute-start.6) | collective-permute-done | bytes 2097184 | tf_op jit(solution)/shard_map/ppermute | solution.py:14
  242.9 3.2 constant_dynamic-update-slice_fusion
  246.2 0.0 copy-start.8
  246.2 0.0 all-gather.4.cloned.1.call-done
  246.2 0.0 all-gather.6.cloned.1.call-done
  246.2 0.0 copy-start.7
  246.2 15.5 %fusion.14 = f32[512,2048]{1,0:T(8,128)S(1)} fusion(bf16[512,4096]{1,0:T(8,128)(2,1)} %all-gather.4.cloned.1.call-done, bf16[4096,2048]{1,0:T(8,128)(2,1)} %all-gather.6.cloned.1.call-done), kind=kOutput, calls=%fused_computation.24 | convolution fusion | flops 8589934592 | bytes 25165824 | tf_op jit(solution)/shard_map/dot_general | solution.py:42
  261.7 0.0 copy-done.8
  261.7 0.0 copy-done.7
  261.7 15.7 %fusion.5 = f32[512,2048]{1,0:T(8,128)} fusion(f32[512,2048]{1,0:T(8,128)S(1)} %fusion.14, bf16[512,2048]{1,0:T(8,128)(2,1)S(1)} %copy-done.8, bf16[512,4096]{1,0:T(8,128)(2,1)S(1)} %copy-done.7, bf16[4096,2048]{1,0:T(8,128)(2,1)} %constant_dynamic-update-slice_fusion), kind=kOutput, calls=%fused_computation.8 | convolution fusion | flops 8604614656 | bytes 31457280 | tf_op jit(solution)/shard_map/dot_general | solution.py:42
  277.4 121.8 %all-gather.8.cloned.1.call-done = bf16[4096,2,2048]{2,1,0:T(2,128)(2,1)} async-done(((bf16[512,2,2048]{2,1,0:T(2,128)(2,1)}), bf16[4096,2,2048]{2,1,0:T(2,128)(2,1)}) %all-gather.8.cloned.1.call-update) | async-done | bytes 33554448 | tf_op jit(solution)/shard_map/all_gather | solution.py:46
  399.2 80.8 %copy.12 = bf16[4096,2,2048]{0,2,1:T(8,128)(2,1)} copy(bf16[4096,2,2048]{2,1,0:T(2,128)(2,1)} %all-gather.8.cloned.1.call-done) | data formatting | bytes 67108864 | tf_op jit(solution)/shard_map/reshape | solution.py:47
  480.0 24.1 %multiply_convert_fusion = bf16[512,2,2048]{2,0,1:T(8,128)(2,1)} fusion(f32[512,2048]{1,0:T(8,128)} %fusion.5, bf16[4096,2,2048]{0,2,1:T(8,128)(2,1)} %copy.12, bf16[512,4096]{1,0:T(8,128)(2,1)} %all-gather.4.cloned.1.call-done), kind=kOutput, calls=%fused_computation.3 | convolution fusion | flops 17184063488 | bytes 46137344 | tf_op jit(solution)/shard_map/dot_general | solution.py:42
  504.1 6.2 copy.11
  510.3 24.2 %convolution_convert_fusion = bf16[4096,4096]{1,0:T(8,128)(2,1)} fusion(bf16[512,4096]{1,0:T(8,128)(2,1)} %all-gather.4.cloned.1.call-done, bf16[512,4096]{0,1:T(8,128)(2,1)} %bitcast.21), kind=kOutput, calls=%fused_computation.2 | convolution fusion | flops 17196646400 | bytes 41943040 | tf_op jit(solution)/shard_map/dot_general | solution.py:55
  534.5 0.0 reduce-scatter.2.cloned.1.call-update
  534.5 205.6 %reduce-scatter.2.cloned.1.call-done = bf16[512,4096]{1,0:T(8,128)(2,1)} async-done(((bf16[4096,4096]{1,0:T(8,128)(2,1)}), bf16[512,4096]{1,0:T(8,128)(2,1)}) %reduce-scatter.2.cloned.1.call-update) | async-done | bytes 4194320 | tf_op jit(solution)/shard_map/reduce_scatter | solution.py:54
  740.1 11.5 %reshape.29 = f32[512,2,2048]{2,1,0:T(2,128)} reshape(bf16[512,4096]{1,0:T(8,128)(2,1)} %reduce-scatter.2.cloned.1.call-done) | data formatting | bytes 12582912 | tf_op jit(solution)/shard_map/reshape | solution.py:62
  (1 shorter events, 0.0 us)
Async XLA Ops:
  6.5 239.6 %all-gather.4.cloned.1.call-start = ((), (), s32[]{:S(2)}) async-start(), calls=%async_computation.1 | async-start | bytes 5242880 | tf_op jit(solution)/shard_map/all_gather | solution.py:36
  10.6 1.6 copy-start
  10.6 235.5 %all-gather.6.cloned.1.call-start = ((), (), s32[]{:S(2)}) async-start(), calls=%async_computation.2 | async-start | bytes 18874368 | tf_op jit(solution)/shard_map/all_gather | solution.py:45
  11.4 387.8 %all-gather.8.cloned.1.call-start = ((), (), s32[]{:S(2)}) async-start(), calls=%async_computation.3 | async-start | bytes 37748736 | tf_op jit(solution)/shard_map/all_gather | solution.py:46
  12.1 728.0 %reduce-scatter.2.cloned.1.call-start = ((), (), s32[]{:S(2)}) async-start(), calls=%async_computation.4 | async-start | bytes 37748736 | tf_op jit(solution)/shard_map/reduce_scatter | solution.py:54
  12.2 47.0 %collective-permute-start = (bf16[512,2048]{1,0:T(8,128)(2,1)S(1)}, bf16[512,2048]{1,0:T(8,128)(2,1)S(1)}, u32[]{:S(2)}, u32[]{:S(2)}) collective-permute-start(bf16[512,2048]{1,0:T(8,128)(2,1)S(1)} %copy-done), channel_id=1, source_target_pairs={{0,4},{4,8},{8,12},{12,16},{16,20},{20,24},{24,28},{28,0},{1,5},{5... | collective-permute-start | bytes 6291464 | tf_op jit(solution)/shard_map/ppermute | solution.py:14
  12.7 47.9 %collective-permute-start.1 = (bf16[512,2048]{1,0:T(8,128)(2,1)S(1)}, bf16[512,2048]{1,0:T(8,128)(2,1)S(1)}, u32[]{:S(2)}, u32[]{:S(2)}) collective-permute-start(bf16[512,2048]{1,0:T(8,128)(2,1)S(1)} %copy-done), channel_id=1, source_target_pairs={{0,28},{4,0},{8,4},{12,8},{16,12},{20,16},{24,20},{28,24},{1,29},{... | collective-permute-start | bytes 6291464 | tf_op jit(solution)/shard_map/ppermute | solution.py:17
  59.2 1.5 copy-start.1
  59.2 46.2 %collective-permute-start.2 = (bf16[512,2048]{1,0:T(8,128)(2,1)S(1)}, bf16[512,2048]{1,0:T(8,128)(2,1)S(1)}, u32[]{:S(2)}, u32[]{:S(2)}) collective-permute-start(bf16[512,2048]{1,0:T(8,128)(2,1)S(1)} %collective-permute-done), channel_id=1, source_target_pairs={{0,4},{4,8},{8,12},{12,16},{16,20},{20,24},{24,28},{28,0},{1,5},{5... | collective-permute-start | bytes 6291464 | tf_op jit(solution)/shard_map/ppermute | solution.py:14
  60.7 44.7 %copy-start.3 = (bf16[512,2048]{1,0:T(8,128)(2,1)}, bf16[512,2048]{1,0:T(8,128)(2,1)S(1)}, u32[]{:S(2)}) copy-start(bf16[512,2048]{1,0:T(8,128)(2,1)S(1)} %collective-permute-done.1) | copy-start | bytes 6291460
  60.7 53.9 %collective-permute-start.3 = (bf16[512,2048]{1,0:T(8,128)(2,1)S(1)}, bf16[512,2048]{1,0:T(8,128)(2,1)}, u32[]{:S(2)}, u32[]{:S(2)}) collective-permute-start(bf16[512,2048]{1,0:T(8,128)(2,1)S(1)} %collective-permute-done.1), channel_id=1, source_target_pairs={{0,28},{4,0},{8,4},{12,8},{16,12},{20,16},{24,20},{28,24},{1,29},{... | collective-permute-start | bytes 6291464 | tf_op jit(solution)/shard_map/ppermute | solution.py:17
  105.4 9.2 %copy-start.5 = (bf16[512,2048]{1,0:T(8,128)(2,1)}, bf16[512,2048]{1,0:T(8,128)(2,1)S(1)}, u32[]{:S(2)}) copy-start(bf16[512,2048]{1,0:T(8,128)(2,1)S(1)} %collective-permute-done.2) | copy-start | bytes 6291460
  105.4 85.1 %collective-permute-start.4 = (bf16[512,2048]{1,0:T(8,128)(2,1)S(1)}, bf16[512,2048]{1,0:T(8,128)(2,1)}, u32[]{:S(2)}, u32[]{:S(2)}) collective-permute-start(bf16[512,2048]{1,0:T(8,128)(2,1)S(1)} %collective-permute-done.2), channel_id=1, source_target_pairs={{0,4},{4,8},{8,12},{12,16},{16,20},{20,24},{24,28},{28,0},{1,5},{5... | collective-permute-start | bytes 6291464 | tf_op jit(solution)/shard_map/ppermute | solution.py:14
  114.6 95.1 %collective-permute-start.5 = (bf16[512,2048]{1,0:T(8,128)(2,1)}, bf16[512,2048]{1,0:T(8,128)(2,1)}, u32[]{:S(2)}, u32[]{:S(2)}) collective-permute-start(bf16[512,2048]{1,0:T(8,128)(2,1)} %collective-permute-done.3), channel_id=1, source_target_pairs={{0,28},{4,0},{8,4},{12,8},{16,12},{20,16},{24,20},{28,24},{1,29},{... | collective-permute-start | bytes 6291464 | tf_op jit(solution)/shard_map/ppermute | solution.py:17
  190.5 52.4 %collective-permute-start.6 = (bf16[512,2048]{1,0:T(8,128)(2,1)}, bf16[512,2048]{1,0:T(8,128)(2,1)}, u32[]{:S(2)}, u32[]{:S(2)}) collective-permute-start(bf16[512,2048]{1,0:T(8,128)(2,1)} %collective-permute-done.4), channel_id=1, source_target_pairs={{0,4},{4,8},{8,12},{12,16},{16,20},{20,24},{24,28},{28,0},{1,5},{5... | collective-permute-start | bytes 6291464 | tf_op jit(solution)/shard_map/ppermute | solution.py:14
  196.5 2.3 copy-start.2
  196.5 3.8 copy-start.4
  198.9 3.0 copy-start.6
  246.2 15.5 %copy-start.8 = (bf16[512,2048]{1,0:T(8,128)(2,1)S(1)}, bf16[512,2048]{1,0:T(8,128)(2,1)}, u32[]{:S(2)}) copy-start(bf16[512,2048]{1,0:T(8,128)(2,1)} %param.11) | copy-start | bytes 6291460
  246.2 15.5 %copy-start.7 = (bf16[512,4096]{1,0:T(8,128)(2,1)S(1)}, bf16[512,4096]{1,0:T(8,128)(2,1)}, u32[]{:S(2)}) copy-start(bf16[512,4096]{1,0:T(8,128)(2,1)} %all-gather.4.cloned.1.call-done) | copy-start | bytes 12582916
Sparse Core Ops, SparseCore 0:
  10.8 83.4 all-gather.3
  96.1 138.6 all-gather.5
  236.7 162.4 all-gather.7
  534.6 205.4 reduce-scatter.1
